TPU v7x, 32 devices: a whole 2x2x4 slice. The times are simulated.
32 devices in a mesh: row: 8 (over z, core), col: 4 (over y, x).
Axes of the slice: x: 2, y: 2, z: 4, core: 2. Of those that a mesh axis runs over, the one named last changes fastest.
Arguments:
- start_panel: bfloat16 [32768, 128], P(('col', 'row')), may hold values from -6 to 6
- block_values: bfloat16 [8, 4, 352, 128, 128], P('row', 'col'), may hold values from -0.078125 to 0.078125
- block_rows: int32 [8, 4, 352], P('row', 'col'), may hold values from 0 to 31, as said below
- block_cols: int32 [8, 4, 352], P('row', 'col'), may hold values from 0 to 63, as said below
- block_counts: int32 [8, 4], P('row', 'col'), may hold values from 141 to 352, as said below
Outputs:
- left_panel: bfloat16 [32768, 128], P(('row', 'col'))
- right_panel: bfloat16 [32768, 128], P(('col', 'row'))
Inputs may be any that keep to these rules, and one draw needn't show every extreme that they name: `block_rows`: block rows lie in 0 to 31 within each tile; low block rows hold more blocks; in every tile some live slot names block row 31. `block_cols`: in every tile some live slot names block column 63; a position may repeat. Only the first block_counts[r, c] slots of tile (r, c) are live; some tile fills all 352 slots.
All inputs are finite; a program needn't handle non-finite values.
Results may differ from a plain program's by a relative error of at most 0.0085.
Values may be sent and summed in bfloat16 or wider, within the bound.
No kernel may reach another device: no remote copies, remote signals or barrier semaphores. Data moves between devices by JAX's collectives and lax.ppermute only.
A program may use at most 128 MiB of HBM per device.

v0:
```python
import jax
import jax.numpy as jnp
from jax import lax
from jax.sharding import PartitionSpec as P


def tile_product(values, index_out, index_in, live_count, panel_in, out_blocks, flipped):
    block_size = values.shape[-1]
    pieces = panel_in.reshape(-1, block_size, panel_in.shape[1])
    selected = jnp.take(pieces, index_in, axis=0)
    if flipped:
        products = jnp.einsum("kij,kip->kjp", values, selected, preferred_element_type=jnp.float32)
    else:
        products = jnp.einsum("kij,kjp->kip", values, selected, preferred_element_type=jnp.float32)
    slots = jnp.arange(values.shape[0], dtype=jnp.int32)
    live = (slots < live_count).astype(jnp.float32)
    targets = jnp.arange(out_blocks, dtype=jnp.int32)
    placement = (targets[:, None] == index_out[None, :]).astype(jnp.float32) * live[None, :]
    summed = jnp.einsum("ok,kip->oip", placement, products, precision=lax.Precision.HIGHEST)
    return summed.reshape(out_blocks * block_size, panel_in.shape[1])


def gram_local(y_rounded, nodes_total):
    return jnp.dot(y_rounded.T, y_rounded, preferred_element_type=jnp.float32) / nodes_total


def apply_factor(y_rounded, gram_total):
    lower = jnp.linalg.cholesky(gram_total)
    identity = jnp.eye(gram_total.shape[0], dtype=jnp.float32)
    inverse = jax.scipy.linalg.solve_triangular(lower, identity, lower=True)
    solved = jnp.dot(y_rounded.astype(jnp.float32), inverse.T, precision=lax.Precision.HIGHEST)
    return solved.astype(jnp.bfloat16)


def global_gram(y_rounded, nodes_total):
    partial_value = gram_local(y_rounded, nodes_total)
    within = lax.psum(partial_value.astype(jnp.bfloat16), "col").astype(jnp.float32)
    return lax.psum(within, "row")


def local(start_panel, block_values, block_rows, block_cols, block_counts):
    group_rows = start_panel.shape[0]
    row_devices = lax.axis_size("row")
    col_devices = lax.axis_size("col")
    nodes_total = group_rows * row_devices * col_devices
    values = block_values[0, 0]
    rows_local = block_rows[0, 0]
    cols_local = block_cols[0, 0]
    live_count = block_counts[0, 0]
    block_size = values.shape[-1]
    row_blocks = group_rows * col_devices // block_size
    col_blocks = group_rows * row_devices // block_size
    column_tile = lax.all_gather(start_panel, "row", axis=0, tiled=True)
    left_partial = tile_product(
        values, rows_local, cols_local, live_count, column_tile, row_blocks, False
    )
    left_group = lax.psum_scatter(left_partial, "col", scatter_dimension=0, tiled=True).astype(
        jnp.bfloat16
    )
    left_panel = apply_factor(left_group, global_gram(left_group, nodes_total))
    row_tile = lax.all_gather(left_panel, "col", axis=0, tiled=True)
    right_partial = tile_product(
        values, cols_local, rows_local, live_count, row_tile, col_blocks, True
    )
    right_group = lax.psum_scatter(right_partial, "row", scatter_dimension=0, tiled=True).astype(
        jnp.bfloat16
    )
    right_panel = apply_factor(right_group, global_gram(right_group, nodes_total))
    return (left_panel, right_panel)


def solution(mesh):
    return jax.shard_map(
        local,
        mesh=mesh,
        in_specs=(
            P(("col", "row"), None),
            P("row", "col", None, None, None),
            P("row", "col", None),
            P("row", "col", None),
            P("row", "col"),
        ),
        out_specs=(P(("row", "col"), None), P(("col", "row"), None)),
        check_vma=False,
    )
```

profile of v0, /device:TPU:0, one launch (start us, length us, event | category | flops | bytes accessed | tf_op | source)
XLA Modules:
  0.0 443.7 jit_solution(17568605688700938867)
XLA Ops:
  10.7 30.8 %all-gather.3.cloned.1.call-done = bf16[8192,128]{1,0:T(8,128)(2,1)} async-done(((bf16[1024,128]{1,0:T(8,128)(2,1)}), bf16[8192,128]{1,0:T(8,128)(2,1)}) %all-gather.3.cloned.1.call-update) | async-done | bytes 2097168 | tf_op jit(solution)/shard_map/all_gather | solution.py:53
  41.5 12.6 %gather_fusion = bf16[352,128,128]{2,1,0:T(8,128)(2,1)} fusion(bf16[64,128,128]{2,1,0:T(8,128)(2,1)} %bitcast.48, s32[1024]{0:T(1024)S(1)} %pad_clamp_fusion.1), kind=kCustom, calls=%fused_computation | custom fusion | bytes 23070080 | tf_op jit(solution)/shard_map/jit(_take)/gather | solution.py:10
  54.1 21.3 %fusion.6 = f32[352,128,128]{2,1,0:T(8,128)} fusion(bf16[1,1,352,128,128]{4,3,2,1,0:T(8,128)(2,1)} %param.9, bf16[352,128,128]{2,1,0:T(8,128)(2,1)} %gather_fusion, pred[352]{0:T(512)(128)(4,1)S(1)} %compare_and_fusion.1), kind=kOutput, calls=%fused_computation.8 | convolution fusion | flops 1482162176 | bytes 46137696 | tf_op jit(solution)/shard_map/kij,kjp->kip/dot_general | solution.py:14
  75.3 23.6 %copy.17 = f32[352,128,128]{1,0,2:T(8,128)} copy(f32[352,128,128]{2,1,0:T(8,128)} %fusion.6) | data formatting | bytes 46137344 | tf_op jit(solution)/shard_map/kij,kjp->kip/dot_general | solution.py:14
  98.9 15.9 %fusion.2 = f32[32,128,128]{2,0,1:T(8,128)S(1)} fusion(f32[352,128,128]{1,0,2:T(8,128)} %copy.17, f32[352]{0:T(512)S(1)} %fusion.40, s32[352]{0:T(512)S(1)} %reduce.4), kind=kOutput, calls=%fused_computation.4 | convolution fusion | flops 2214615040 | bytes 25168640 | tf_op jit(solution)/shard_map/ok,kip->oip/dot_general | solution.py:19
  114.8 2.6 copy.11
  117.4 34.7 %reduce-scatter.3.cloned.1.call-done = f32[1024,128]{1,0:T(8,128)} async-done(((f32[4096,128]{1,0:T(8,128)}), f32[1024,128]{1,0:T(8,128)}) %reduce-scatter.3.cloned.1.call-update) | async-done | bytes 524304 | tf_op jit(solution)/shard_map/reduce_scatter | solution.py:57
  153.6 15.4 %psum.28 = bf16[128,128]{0,1:T(8,128)(2,1)S(1)} all-reduce(bf16[128,128]{0,1:T(8,128)(2,1)S(1)} %fusion.14), channel_id=1, replica_groups=mesh['row'=8,'col'=4] {'col'}, use_global_device_ids=true, to_apply=%region_1.2 | all-reduce | flops 16384 | bytes 65536 | tf_op jit(solution)/shard_map/psum | solution.py:37
  169.0 26.8 %all-reduce.2 = f32[128,128]{0,1:T(8,128)S(1)} all-reduce(bf16[128,128]{0,1:T(8,128)(2,1)S(1)} %psum.28), channel_id=1, replica_groups=mesh['row'=8,'col'=4] {'row'}, use_global_device_ids=true, to_apply=%region_2.3 | all-reduce | flops 16384 | bytes 98304 | tf_op jit(solution)/shard_map/psum | solution.py:38
  195.9 11.7 %cholesky.44 = f32[128,128]{1,0:T(8,128)S(1)} custom-call(f32[128,128]{1,0:T(8,128)S(1)} %fusion.31), custom_call_target="Cholesky" | custom-call | tf_op jit(solution)/shard_map/jit(cholesky)/cholesky | solution.py:28
  209.0 9.8 %custom-call.6 = f32[1,128,128]{1,2,0:T(8,128)S(1)} custom-call(f32[1,128,128]{2,1,0:T(8,128)S(1)} %fusion.26), custom_call_target="InvertDiagBlocksLowerTriangular" | custom-call | tf_op jit(solution)/shard_map/jit(_solve_triangular)/triangular_solve | solution.py:30
  219.1 2.1 convolution_convert_fusion.1
  221.5 23.5 %all-gather.5.cloned.1.call-done = bf16[4096,128]{1,0:T(8,128)(2,1)} async-done(((bf16[1024,128]{1,0:T(8,128)(2,1)}), bf16[4096,128]{1,0:T(8,128)(2,1)}) %all-gather.5.cloned.1.call-update) | async-done | bytes 1048592 | tf_op jit(solution)/shard_map/all_gather | solution.py:61
  245.0 12.2 %gather_fusion.1 = bf16[352,128,128]{2,1,0:T(8,128)(2,1)} fusion(bf16[32,128,128]{2,1,0:T(8,128)(2,1)} %bitcast.47, s32[1024]{0:T(1024)S(1)} %pad_clamp_fusion), kind=kCustom, calls=%fused_computation.1 | custom fusion | bytes 23070080 | tf_op jit(solution)/shard_map/jit(_take)/gather | solution.py:10
  257.2 14.6 %fusion.4 = f32[352,128,128]{2,1,0:T(8,128)} fusion(bf16[1,1,352,128,128]{4,3,2,1,0:T(8,128)(2,1)} %param.9, bf16[352,128,128]{2,1,0:T(8,128)(2,1)} %gather_fusion.1, pred[352]{0:T(512)(128)(4,1)S(1)} %compare_and_fusion), kind=kOutput, calls=%fused_computation.6 | convolution fusion | flops 1482162176 | bytes 46137696 | tf_op jit(solution)/shard_map/kij,kip->kjp/dot_general | solution.py:12
  271.8 23.6 %copy.19 = f32[352,128,128]{1,0,2:T(8,128)} copy(f32[352,128,128]{2,1,0:T(8,128)} %fusion.4) | data formatting | bytes 46137344 | tf_op jit(solution)/shard_map/kij,kip->kjp/dot_general | solution.py:12
  295.3 17.3 %fusion = f32[64,128,128]{2,0,1:T(8,128)S(1)} fusion(f32[352,128,128]{1,0,2:T(8,128)} %copy.19, f32[352]{0:T(512)S(1)} %fusion.40, s32[352]{0:T(512)S(1)} %reduce.5), kind=kOutput, calls=%fused_computation.2 | convolution fusion | flops 4429230080 | bytes 27265792 | tf_op jit(solution)/shard_map/ok,kip->oip/dot_general | solution.py:19
  312.7 4.4 copy.14
  317.0 50.1 %reduce-scatter.5.cloned.1.call-done = f32[1024,128]{1,0:T(8,128)} async-done(((f32[8192,128]{1,0:T(8,128)}), f32[1024,128]{1,0:T(8,128)}) %reduce-scatter.5.cloned.1.call-update) | async-done | bytes 524304 | tf_op jit(solution)/shard_map/reduce_scatter | solution.py:65
  368.6 16.5 %psum.30 = bf16[128,128]{0,1:T(8,128)(2,1)S(1)} all-reduce(bf16[128,128]{0,1:T(8,128)(2,1)S(1)} %fusion.15), channel_id=1, replica_groups=mesh['row'=8,'col'=4] {'col'}, use_global_device_ids=true, to_apply=%region_6.9 | all-reduce | flops 16384 | bytes 65536 | tf_op jit(solution)/shard_map/psum | solution.py:37
  385.1 26.4 %all-reduce.3 = f32[128,128]{0,1:T(8,128)S(1)} all-reduce(bf16[128,128]{0,1:T(8,128)(2,1)S(1)} %psum.30), channel_id=1, replica_groups=mesh['row'=8,'col'=4] {'row'}, use_global_device_ids=true, to_apply=%region_7.10 | all-reduce | flops 16384 | bytes 98304 | tf_op jit(solution)/shard_map/psum | solution.py:38
  411.6 11.7 %cholesky.55 = f32[128,128]{1,0:T(8,128)S(1)} custom-call(f32[128,128]{1,0:T(8,128)S(1)} %fusion.29), custom_call_target="Cholesky" | custom-call | tf_op jit(solution)/shard_map/jit(cholesky)/cholesky | solution.py:28
  424.7 9.8 %custom-call.7 = f32[1,128,128]{1,2,0:T(8,128)S(1)} custom-call(f32[1,128,128]{2,1,0:T(8,128)S(1)} %fusion.27), custom_call_target="InvertDiagBlocksLowerTriangular" | custom-call | tf_op jit(solution)/shard_map/jit(_solve_triangular)/triangular_solve | solution.py:30
  434.8 2.1 convolution_convert_fusion
  (33 shorter events, 9.6 us)
Async XLA Ops:
  7.2 34.3 %all-gather.3.cloned.1.call-start = ((), (), s32[]{:S(2)}) async-start(), calls=%async_computation.2 | async-start | bytes 2359296 | tf_op jit(solution)/shard_map/all_gather | solution.py:53
  7.9 144.2 %reduce-scatter.3.cloned.1.call-start = ((), (), s32[]{:S(2)}) async-start(), calls=%async_computation.3 | async-start | bytes 2621440 | tf_op jit(solution)/shard_map/reduce_scatter | solution.py:57
  98.9 122.5 %copy-start = (s32[1,1,352]{2,1,0:T(1,128)S(1)}, s32[1,1,352]{2,1,0:T(1,128)}, u32[]{:S(2)}) copy-start(s32[1,1,352]{2,1,0:T(1,128)} %param.10) | copy-start | bytes 4228
  117.3 127.7 %all-gather.5.cloned.1.call-start = ((), (), s32[]{:S(2)}) async-start(), calls=%async_computation.4 | async-start | bytes 1310720 | tf_op jit(solution)/shard_map/all_gather | solution.py:61
  221.2 145.9 %reduce-scatter.5.cloned.1.call-start = ((), (), s32[]{:S(2)}) async-start(), calls=%async_computation.5 | async-start | bytes 4718592 | tf_op jit(solution)/shard_map/reduce_scatter | solution.py:65
Sparse Core Ops, SparseCore 0:
  9.6 31.8 all-gather.2
  117.5 34.5 reduce-scatter.2
  221.3 23.6 all-gather.4
  317.2 49.9 reduce-scatter.4
where the time goes:
time: 452 us; the launch traced here: 444 us
  waiting for transfers between devices  140 us (31%)
  blocking collectives  85.1 us (19%)
  local copies, waits for them, and re-layouts  79 us (17%)
  matrix products  76.8 us (17%)
  other arithmetic  47.9 us (11%)
  between operations  14.8 us (3%)
    psum x2, blocking collectives, global_gram(): return lax.psum(within, 'row')  53.1 us
    reduce_scatter x1, waiting for transfers between devices, local(): lax.psum_scatter(right_partial, 'row', scatter_dimension=0, tiled=True)  50.1 us
    reduce_scatter x1, waiting for transfers between devices, local(): lax.psum_scatter(left_partial, 'col', scatter_dimension=0, tiled=True)  34.7 us
    dot_general x2, matrix products, tile_product(): jnp.einsum('ok,kip->oip', placement, products, precision=lax.Precision.HI...  33.2 us
    psum x2, blocking collectives, global_gram(): lax.psum(partial_value.astype(jnp.bfloat16), 'col').astype(jnp.float32)  31.9 us
    all_gather x1, waiting for transfers between devices, local(): column_tile = lax.all_gather(start_panel, 'row', axis=0, tiled=True)  30.8 us
    another operation x6, other arithmetic, apply_factor(): lower = jnp.linalg.cholesky(gram_total)  24.8 us
    gather x2, local copies, waits for them, and re-layouts, tile_product(): selected = jnp.take(pieces, index_in, axis=0)  24.8 us
  transfers between devices with their start and end apart: 4, of which 4 were waited for; matrix products, arithmetic and copies ran while one was open for 0% of the time, Pallas kernels for 0%

commit v1 on v0

--- a/solution.py
+++ b/solution.py
@@ -2,6 +2,8 @@
 import jax.numpy as jnp
 from jax import lax
 from jax.sharding import PartitionSpec as P
+
+patches_track = lambda v0: jnp.sum(lax.all_gather(v0, "col"), axis=0)
 
 
 def tile_product(values, index_out, index_in, live_count, panel_in, out_blocks, flipped):
@@ -34,7 +36,7 @@
 
 def global_gram(y_rounded, nodes_total):
     partial_value = gram_local(y_rounded, nodes_total)
-    within = lax.psum(partial_value.astype(jnp.bfloat16), "col").astype(jnp.float32)
+    within = patches_track(partial_value.astype(jnp.bfloat16)).astype(jnp.float32)
     return lax.psum(within, "row")
 
 

time: 452 us -> 438 us (0.969)
  blocking collectives: 85.1 us -> 70.7 us
    psum x2 -> x0, blocking collectives: 31.9 us -> none  [global_gram(): lax.psum(partial_value.astype(jnp.bfloat16), 'col').astype(jnp.float32)]
    all_gather x0 -> x2, blocking collectives: none -> 16.9 us  [patches_track = lambda v0: jnp.sum(lax.all_gather(v0, 'col'), axis=0)]
  transfers between devices with their start and end apart: 4 -> 4, of which waited for: 4 -> 4; matrix products, arithmetic and copies ran while one was open for 0% -> 1% of each run, Pallas kernels for 0% -> 0%
where the time goes in v1:
time: 438 us; the launch traced here: 430 us
  waiting for transfers between devices  140 us (32%)
  local copies, waits for them, and re-layouts  79.2 us (18%)
  matrix products  76.8 us (18%)
  blocking collectives  70.7 us (16%)
  other arithmetic  47.9 us (11%)
  between operations  14.8 us (3%)
    psum x2, blocking collectives, global_gram(): return lax.psum(within, 'row')  53.8 us
    reduce_scatter x1, waiting for transfers between devices, local(): lax.psum_scatter(right_partial, 'row', scatter_dimension=0, tiled=True)  50.1 us
    reduce_scatter x1, waiting for transfers between devices, local(): lax.psum_scatter(left_partial, 'col', scatter_dimension=0, tiled=True)  34.7 us
    dot_general x2, matrix products, tile_product(): jnp.einsum('ok,kip->oip', placement, products, precision=lax.Precision.HI...  33.2 us
    all_gather x1, waiting for transfers between devices, local(): column_tile = lax.all_gather(start_panel, 'row', axis=0, tiled=True)  30.8 us
    another operation x6, other arithmetic, apply_factor(): lower = jnp.linalg.cholesky(gram_total)  24.8 us
    gather x2, local copies, waits for them, and re-layouts, tile_product(): selected = jnp.take(pieces, index_in, axis=0)  24.8 us
    all_gather x1, waiting for transfers between devices, local(): row_tile = lax.all_gather(left_panel, 'col', axis=0, tiled=True)  23.6 us
  transfers between devices with their start and end apart: 4, of which 4 were waited for; matrix products, arithmetic and copies ran while one was open for 1% of the time, Pallas kernels for 0%

profile of v1, /device:TPU:0, one launch (start us, length us, event | category | flops | bytes accessed | tf_op | source)
XLA Modules:
  0.0 429.6 jit_solution(16980808959628491625)
XLA Ops:
  10.7 30.8 %all-gather.5.cloned.1.call-done = bf16[8192,128]{1,0:T(8,128)(2,1)} async-done(((bf16[1024,128]{1,0:T(8,128)(2,1)}), bf16[8192,128]{1,0:T(8,128)(2,1)}) %all-gather.5.cloned.1.call-update) | async-done | bytes 2097168 | tf_op jit(solution)/shard_map/all_gather | solution.py:55
  41.5 12.6 %gather_fusion = bf16[352,128,128]{2,1,0:T(8,128)(2,1)} fusion(bf16[64,128,128]{2,1,0:T(8,128)(2,1)} %bitcast.54, s32[1024]{0:T(1024)S(1)} %pad_clamp_fusion.1), kind=kCustom, calls=%fused_computation | custom fusion | bytes 23070080 | tf_op jit(solution)/shard_map/jit(_take)/gather | solution.py:12
  54.1 21.3 %fusion.8 = f32[352,128,128]{1,2,0:T(8,128)} fusion(bf16[1,1,352,128,128]{4,3,2,1,0:T(8,128)(2,1)} %param.9, bf16[352,128,128]{2,1,0:T(8,128)(2,1)} %gather_fusion, pred[352]{0:T(512)(128)(4,1)S(1)} %compare_and_fusion.1), kind=kOutput, calls=%fused_computation.10 | convolution fusion | flops 1482162176 | bytes 46137696 | tf_op jit(solution)/shard_map/kij,kjp->kip/dot_general | solution.py:16
  75.3 23.6 %copy.22 = f32[352,128,128]{2,0,1:T(8,128)} copy(f32[352,128,128]{1,2,0:T(8,128)} %fusion.8) | data formatting | bytes 46137344 | tf_op jit(solution)/shard_map/kij,kjp->kip/dot_general | solution.py:16
  98.9 15.9 %fusion.39 = f32[32,128,128]{2,0,1:T(8,128)S(1)} fusion(f32[352,128,128]{2,0,1:T(8,128)} %copy.22, f32[352]{0:T(512)S(1)} %fusion.48, s32[352]{0:T(512)S(1)} %reduce.6), kind=kOutput, calls=%fused_computation.46 | convolution fusion | flops 2214615040 | bytes 25168640 | tf_op jit(solution)/shard_map/ok,kip->oip/dot_general | solution.py:21
  114.8 2.6 copy.23
  117.4 34.7 %reduce-scatter.3.cloned.1.call-done = f32[1024,128]{1,0:T(8,128)} async-done(((f32[4096,128]{1,0:T(8,128)}), f32[1024,128]{1,0:T(8,128)}) %reduce-scatter.3.cloned.1.call-update) | async-done | bytes 524304 | tf_op jit(solution)/shard_map/reduce_scatter | solution.py:59
  153.6 8.5 %all-gather = bf16[512,128]{1,0:T(8,128)(2,1)S(1)} all-gather(bf16[128,128]{1,0:T(8,128)(2,1)S(1)} %fusion.20), channel_id=2, replica_groups=mesh['row'=8,'col'=4] {'col'}, dimensions={0}, use_global_device_ids=true | all-gather | bytes 163840 | tf_op jit(solution)/shard_map/all_gather | solution.py:6
  162.2 27.2 %all-reduce.2 = f32[128,128]{0,1:T(8,128)S(1)} all-reduce(bf16[128,128]{0,1:T(8,128)(2,1)S(1)} %copy.24), channel_id=1, replica_groups=mesh['row'=8,'col'=4] {'row'}, use_global_device_ids=true, to_apply=%region_2.3 | all-reduce | flops 16384 | bytes 98304 | tf_op jit(solution)/shard_map/psum | solution.py:40
  189.5 11.7 %cholesky.44 = f32[128,128]{1,0:T(8,128)S(1)} custom-call(f32[128,128]{1,0:T(8,128)S(1)} %fusion.38), custom_call_target="Cholesky" | custom-call | tf_op jit(solution)/shard_map/jit(cholesky)/cholesky | solution.py:30
  202.6 9.8 %custom-call.6 = f32[1,128,128]{1,2,0:T(8,128)S(1)} custom-call(f32[1,128,128]{2,1,0:T(8,128)S(1)} %fusion.33), custom_call_target="InvertDiagBlocksLowerTriangular" | custom-call | tf_op jit(solution)/shard_map/jit(_solve_triangular)/triangular_solve | solution.py:32
  212.7 2.1 convolution_convert_fusion.1
  215.1 23.6 %all-gather.7.cloned.1.call-done = bf16[4096,128]{1,0:T(8,128)(2,1)} async-done(((bf16[1024,128]{1,0:T(8,128)(2,1)}), bf16[4096,128]{1,0:T(8,128)(2,1)}) %all-gather.7.cloned.1.call-update) | async-done | bytes 1048592 | tf_op jit(solution)/shard_map/all_gather | solution.py:63
  238.7 12.2 %gather_fusion.1 = bf16[352,128,128]{2,1,0:T(8,128)(2,1)} fusion(bf16[32,128,128]{2,1,0:T(8,128)(2,1)} %bitcast.53, s32[1024]{0:T(1024)S(1)} %pad_clamp_fusion), kind=kCustom, calls=%fused_computation.1 | custom fusion | bytes 23070080 | tf_op jit(solution)/shard_map/jit(_take)/gather | solution.py:12
  250.9 14.6 %fusion.13 = f32[352,128,128]{1,2,0:T(8,128)} fusion(bf16[1,1,352,128,128]{4,3,2,1,0:T(8,128)(2,1)} %param.9, bf16[352,128,128]{2,1,0:T(8,128)(2,1)} %gather_fusion.1, pred[352]{0:T(512)(128)(4,1)S(1)} %compare_and_fusion), kind=kOutput, calls=%fused_computation.11 | convolution fusion | flops 1482162176 | bytes 46137696 | tf_op jit(solution)/shard_map/kij,kip->kjp/dot_general | solution.py:14
  265.5 23.6 %copy.27 = f32[352,128,128]{2,0,1:T(8,128)} copy(f32[352,128,128]{1,2,0:T(8,128)} %fusion.13) | data formatting | bytes 46137344 | tf_op jit(solution)/shard_map/kij,kip->kjp/dot_general | solution.py:14
  289.1 17.3 %fusion.26 = f32[64,128,128]{2,0,1:T(8,128)S(1)} fusion(f32[352,128,128]{2,0,1:T(8,128)} %copy.27, f32[352]{0:T(512)S(1)} %fusion.48, s32[352]{0:T(512)S(1)} %reduce.7), kind=kOutput, calls=%fused_computation.24 | convolution fusion | flops 4429230080 | bytes 27265792 | tf_op jit(solution)/shard_map/ok,kip->oip/dot_general | solution.py:21
  306.4 4.4 %copy.28 = f32[64,128,128]{2,1,0:T(8,128)} copy(f32[64,128,128]{2,0,1:T(8,128)S(1)} %fusion.26) | data formatting | bytes 8388608 | tf_op jit(solution)/shard_map/ok,kip->oip/dot_general | solution.py:21
  310.8 50.1 %reduce-scatter.5.cloned.1.call-done = f32[1024,128]{1,0:T(8,128)} async-done(((f32[8192,128]{1,0:T(8,128)}), f32[1024,128]{1,0:T(8,128)}) %reduce-scatter.5.cloned.1.call-update) | async-done | bytes 524304 | tf_op jit(solution)/shard_map/reduce_scatter | solution.py:67
  362.3 8.4 %all-gather.1 = bf16[512,128]{1,0:T(8,128)(2,1)S(1)} all-gather(bf16[128,128]{1,0:T(8,128)(2,1)S(1)} %fusion.21), channel_id=3, replica_groups=mesh['row'=8,'col'=4] {'col'}, dimensions={0}, use_global_device_ids=true | all-gather | bytes 163840 | tf_op jit(solution)/shard_map/all_gather | solution.py:6
  370.9 26.6 %all-reduce.3 = f32[128,128]{0,1:T(8,128)S(1)} all-reduce(bf16[128,128]{0,1:T(8,128)(2,1)S(1)} %copy.29), channel_id=1, replica_groups=mesh['row'=8,'col'=4] {'row'}, use_global_device_ids=true, to_apply=%region_7.10 | all-reduce | flops 16384 | bytes 98304 | tf_op jit(solution)/shard_map/psum | solution.py:40
  397.6 11.7 %cholesky.55 = f32[128,128]{1,0:T(8,128)S(1)} custom-call(f32[128,128]{1,0:T(8,128)S(1)} %fusion.36), custom_call_target="Cholesky" | custom-call | tf_op jit(solution)/shard_map/jit(cholesky)/cholesky | solution.py:30
  410.7 9.8 %custom-call.7 = f32[1,128,128]{1,2,0:T(8,128)S(1)} custom-call(f32[1,128,128]{2,1,0:T(8,128)S(1)} %fusion.34), custom_call_target="InvertDiagBlocksLowerTriangular" | custom-call | tf_op jit(solution)/shard_map/jit(_solve_triangular)/triangular_solve | solution.py:32
  420.8 2.1 convolution_convert_fusion
  (37 shorter events, 9.9 us)
Async XLA Ops:
  7.2 34.3 %all-gather.5.cloned.1.call-start = ((), (), s32[]{:S(2)}) async-start(), calls=%async_computation.2 | async-start | bytes 2359296 | tf_op jit(solution)/shard_map/all_gather | solution.py:55
  7.9 144.2 %reduce-scatter.3.cloned.1.call-start = ((), (), s32[]{:S(2)}) async-start(), calls=%async_computation.3 | async-start | bytes 2621440 | tf_op jit(solution)/shard_map/reduce_scatter | solution.py:59
  98.9 116.2 %copy-start = (s32[1,1,352]{2,1,0:T(1,128)S(1)}, s32[1,1,352]{2,1,0:T(1,128)}, u32[]{:S(2)}) copy-start(s32[1,1,352]{2,1,0:T(1,128)} %param.10) | copy-start | bytes 4228
  117.3 121.4 %all-gather.7.cloned.1.call-start = ((), (), s32[]{:S(2)}) async-start(), calls=%async_computation.4 | async-start | bytes 1310720 | tf_op jit(solution)/shard_map/all_gather | solution.py:63
  214.9 146.0 %reduce-scatter.5.cloned.1.call-start = ((), (), s32[]{:S(2)}) async-start(), calls=%async_computation.5 | async-start | bytes 4718592 | tf_op jit(solution)/shard_map/reduce_scatter | solution.py:67
Sparse Core Ops, SparseCore 0:
  9.6 31.8 all-gather.4
  117.5 34.5 reduce-scatter.2
  215.0 23.7 all-gather.6
  310.9 49.9 reduce-scatter.4
